TPU v7x, 128 devices: a whole 4x4x4 slice. The times are simulated.
128 devices in a mesh: mem: 16 (over z, x_hi, core), lev: 8 (over y, x_lo).
Axes of the slice: x: 4 (x_hi: 2, x_lo: 2; x = x_hi * 2 + x_lo), y: 4, z: 4, core: 2. Of those that a mesh axis runs over, the one named last changes fastest.
Arguments:
- control: float32 [16, 128, 128, 256], P('mem', 'lev'), may hold values from -6 to 6
- diffusivity: float32 [128, 128, 256], P('lev'), may hold values from 0.02 to 0.24
- perturb: float32 [16, 49152, 128], P('mem', 'lev'), may hold values from -6 to 6
- vertical_filter: float32 [128, 128], replicated, may hold values from -0.5 to 0.5
- sub_widths: int32 [8], replicated, may hold values from 1 to 6144, 32768 in all
- obs_raw: int32 [8, 6144], P('lev'), may hold values from 0 to 1048575
- obs_counts: int32 [8], replicated, may hold values from 1 to 6144, 43008 in all
- obs_rinv: float32 [8, 6144, 128], P('lev'), may hold values from 0.3 to 3
Outputs:
- ensemble_term: float32 [16, 128, 128, 256], P('mem', 'lev')
Inputs may be any that keep to these rules, and one draw needn't show every extreme that they name: `sub_widths`: the widths sum to 32768; the largest is exactly 6144. `obs_counts`: the counts sum to 43008; the largest is exactly 6144.
All inputs are finite; a program needn't handle non-finite values.
Results may differ from a plain program's by a relative error of at most 0.00011.
Values sent between devices are 32-bit elements; how exact they have to be, the bound alone decides.
A program may use at most 192 MiB of HBM per device.

v0:
```python
import functools

import jax
import jax.numpy as jnp
from jax import lax
from jax.experimental import pallas as pl
from jax.experimental.pallas import tpu as pltpu
from jax.sharding import PartitionSpec as P

STEPS = 4
LANES = 128


def lane_index(shape):
    return lax.broadcasted_iota(jnp.int32, shape, len(shape) - 1)


def make_faces(diff_ref, face_x, face_y, size_x):
    levels = face_x.shape[1]
    lane = lane_index((levels, LANES))
    load, _ = rows_access(diff_ref, size_x, levels)

    def step(i, here):
        k0, k1 = here
        after = jnp.minimum(i + 1, size_x - 1)
        n0, n1 = load(after, 0), load(after, 1)
        inner = jnp.where(i < size_x - 1, 0.5, 0.0)
        face_x[2 * i] = inner * (k0 + n0)
        face_x[2 * i + 1] = inner * (k1 + n1)
        r0, r1 = pltpu.roll(k0, LANES - 1, 1), pltpu.roll(k1, LANES - 1, 1)
        face_y[2 * i] = 0.5 * (k0 + jnp.where(lane == LANES - 1, r1, r0))
        face_y[2 * i + 1] = jnp.where(lane == LANES - 1, 0.0, 0.5 * (k1 + r1))
        return n0, n1

    lax.fori_loop(0, size_x, step, (load(0, 0), load(0, 1)))


def diffuse_pass(load, store, face_x, face_y, size_x):
    levels = face_x.shape[1]
    lane = lane_index((levels, LANES))
    last, first = lane == LANES - 1, lane == 0
    zero = jnp.zeros((levels, LANES), jnp.float32)

    def step(i, carry):
        v0, v1, above0, above1 = carry
        after = jnp.minimum(i + 1, size_x - 1)
        n0, n1 = load(after, 0), load(after, 1)
        x0 = face_x[2 * i] * (n0 - v0)
        x1 = face_x[2 * i + 1] * (n1 - v1)
        r0, r1 = pltpu.roll(v0, LANES - 1, 1), pltpu.roll(v1, LANES - 1, 1)
        y0 = face_y[2 * i] * (jnp.where(last, r1, r0) - v0)
        y1 = face_y[2 * i + 1] * (r1 - v1)
        b0, b1 = pltpu.roll(y0, 1, 1), pltpu.roll(y1, 1, 1)
        store(i, 0, v0 + (x0 - above0) + (y0 - jnp.where(first, b1, b0)))
        store(i, 1, v1 + (x1 - above1) + (y1 - jnp.where(first, b0, b1)))
        return n0, n1, x0, x1

    lax.fori_loop(0, size_x, step, (load(0, 0), load(0, 1), zero, zero), unroll=2)


def flat_access(ref):
    def load(i, half):
        return ref[2 * i + half]

    def store(i, half, value):
        ref[2 * i + half] = value

    return load, store


def rows_access(ref, size_x, levels):
    def load(i, half):
        return ref[half, pl.ds(i, levels, stride=size_x), :]

    def store(i, half, value):
        ref[half, pl.ds(i, levels, stride=size_x), :] = value

    return load, store


def halves(array, scratch, sems):
    return [
        pltpu.make_async_copy(array.at[:, pl.ds(h * LANES, LANES)], scratch.at[h], sems.at[h])
        for h in range(2)
    ]


def forward_kernel(
    size_x, starts, control_in, diff_in, pieces, face_x, face_y, one, two, control, diff, sems
):
    groups, levels, capacity = pieces.shape
    tiles = 2 * size_x
    diff_copies = halves(diff_in, diff, sems.at[0])
    control_copies = halves(control_in, control, sems.at[1])
    for copy in diff_copies + control_copies:
        copy.start()
    for copy in diff_copies:
        copy.wait()
    make_faces(diff, face_x, face_y, size_x)
    for copy in control_copies:
        copy.wait()
    load_in, _ = rows_access(control, size_x, levels)
    load_one, store_one = flat_access(one)
    load_two, store_two = flat_access(two)
    diffuse_pass(load_in, store_one, face_x, face_y, size_x)
    diffuse_pass(load_one, store_two, face_x, face_y, size_x)
    diffuse_pass(load_two, store_one, face_x, face_y, size_x)
    diffuse_pass(load_one, store_two, face_x, face_y, size_x)
    lane = lane_index((levels, LANES))
    for group in range(groups):
        start = starts[group]
        tile, shift = start // LANES, start % LANES
        keep = lane < LANES - shift
        back = (LANES - shift) % LANES

        def window(q, here):
            after = pltpu.roll(two[jnp.minimum(tile + q + 1, tiles - 1)], back, 1)
            at = pl.multiple_of(q * LANES, LANES)
            pieces[group, :, pl.ds(at, LANES)] = jnp.where(keep, here, after)
            return after

        begin = pltpu.roll(two[jnp.minimum(tile, tiles - 1)], back, 1)
        lax.fori_loop(0, capacity // LANES, window, begin, unroll=4)


def backward_kernel(
    size_x, starts, blocks, diff_in, out_to, face_x, face_y, one, two, out, diff, sems
):
    groups, levels, capacity = blocks.shape
    diff_copies = halves(diff_in, diff, sems.at[0])
    for copy in diff_copies:
        copy.start()
    for copy in diff_copies:
        copy.wait()
    make_faces(diff, face_x, face_y, size_x)
    lane = lane_index((levels, LANES))
    for group in range(groups):
        start = starts[group]
        tile, shift = start // LANES, start % LANES
        keep = lane >= shift

        def place(q, before):
            at = pl.multiple_of(q * LANES, LANES)
            here = pltpu.roll(blocks[group, :, pl.ds(at, LANES)], shift, 1)
            one[tile + q] = jnp.where(keep, here, before)
            return here

        tail = lax.fori_loop(0, capacity // LANES, place, one[tile], unroll=4)
        one[tile + capacity // LANES] = tail
    load_one, store_one = flat_access(one)
    load_two, store_two = flat_access(two)
    _, store_out = rows_access(out, size_x, levels)
    diffuse_pass(load_one, store_two, face_x, face_y, size_x)
    diffuse_pass(load_two, store_one, face_x, face_y, size_x)
    diffuse_pass(load_one, store_two, face_x, face_y, size_x)
    diffuse_pass(load_two, store_out, face_x, face_y, size_x)
    copies = [
        pltpu.make_async_copy(out.at[h], out_to.at[:, pl.ds(h * LANES, LANES)], sems.at[1, h])
        for h in range(2)
    ]
    for copy in copies:
        copy.start()
    for copy in copies:
        copy.wait()


def split_two(values):
    high = values.astype(jnp.bfloat16)
    low = (values - high.astype(jnp.float32)).astype(jnp.bfloat16)
    return high, low


def weights_kernel(base, slots, rinv, out):
    rows = out.shape[0]
    total = rinv.shape[0]
    block = 1024
    acc = jnp.zeros((rows, 2 * LANES), jnp.float32)
    here = base[0] + lax.broadcasted_iota(jnp.int32, (rows, block), 0)
    for k in range(total // block):
        high, low = split_two(rinv[k * block : (k + 1) * block, :])
        chosen = (here == slots[:, k * block : (k + 1) * block]).astype(jnp.bfloat16)
        both = jnp.concatenate([high, low], axis=1)
        acc += jnp.dot(chosen, both, preferred_element_type=jnp.float32)
    out[...] = acc[:, :LANES] + acc[:, LANES:]


SMEM = pl.BlockSpec(memory_space=pltpu.SMEM)
VMEM = pl.BlockSpec(memory_space=pltpu.VMEM)
ANY = pl.BlockSpec(memory_space=pl.ANY)
LIMIT = 60 * 1024 * 1024


def body(control, diffusivity, perturb, vertical_filter, sub_widths, obs_raw, obs_counts, obs_rinv):
    members, levels, size_x, size_y = control.shape
    capacity = perturb.shape[1]
    groups = sub_widths.shape[0]
    tiles = 2 * size_x
    highest = lax.Precision.HIGHEST
    starts = jnp.cumsum(sub_widths) - sub_widths
    diff = diffusivity.reshape(levels * size_x, size_y)
    scratch = [
        pltpu.VMEM((tiles, levels, LANES), jnp.float32),
        pltpu.VMEM((tiles, levels, LANES), jnp.float32),
        pltpu.VMEM((tiles + capacity // LANES + 1, levels, LANES), jnp.float32),
        pltpu.VMEM((tiles, levels, LANES), jnp.float32),
        pltpu.VMEM((2, levels * size_x, LANES), jnp.float32),
        pltpu.VMEM((2, levels * size_x, LANES), jnp.float32),
        pltpu.SemaphoreType.DMA((2, 2)),
    ]
    pieces = pl.pallas_call(
        functools.partial(forward_kernel, size_x),
        out_shape=jax.ShapeDtypeStruct((groups, levels, capacity), jnp.float32),
        in_specs=[SMEM, ANY, ANY],
        out_specs=VMEM,
        scratch_shapes=scratch,
        compiler_params=pltpu.CompilerParams(vmem_limit_bytes=LIMIT),
        name="forward",
    )(starts, control.reshape(levels * size_x, size_y), diff)

    column_form = lax.all_to_all(pieces, "lev", split_axis=0, concat_axis=0, tiled=True)
    column_form = column_form.reshape(groups * levels, capacity)
    filtered = jnp.einsum("ks,lk->sl", column_form, vertical_filter, precision=highest)

    position = lax.axis_index("lev")
    width = sub_widths[position]
    slots = obs_raw % width
    live = jnp.arange(obs_raw.shape[1], dtype=jnp.int32)[None] < obs_counts[position]
    slots = jnp.where(live, slots, -1)
    owned = capacity // lax.axis_size("mem")
    base = (lax.axis_index("mem") * owned).astype(jnp.int32).reshape(1)
    weight = pl.pallas_call(
        weights_kernel,
        out_shape=jax.ShapeDtypeStruct((owned, groups * levels), jnp.float32),
        in_specs=[SMEM, VMEM, VMEM],
        out_specs=VMEM,
        compiler_params=pltpu.CompilerParams(vmem_limit_bytes=LIMIT),
        name="weights",
    )(base, slots, obs_rinv[0])

    part = lax.psum_scatter(perturb[0] * filtered, "mem", scatter_dimension=0, tiled=True)
    adjoint = lax.all_gather(part * weight, "mem", axis=0, tiled=True)
    back = jnp.einsum("sl,lk->ks", perturb[0] * adjoint, vertical_filter, precision=highest)
    blocks = lax.all_to_all(
        back.reshape(groups, levels, capacity), "lev", split_axis=0, concat_axis=0, tiled=True
    )

    out = pl.pallas_call(
        functools.partial(backward_kernel, size_x),
        out_shape=jax.ShapeDtypeStruct((levels * size_x, size_y), jnp.float32),
        in_specs=[SMEM, VMEM, ANY],
        out_specs=ANY,
        scratch_shapes=scratch,
        compiler_params=pltpu.CompilerParams(vmem_limit_bytes=LIMIT),
        name="backward",
    )(starts, blocks, diff)
    return out.reshape(control.shape)


def solution(mesh):
    return jax.shard_map(
        body,
        mesh=mesh,
        in_specs=(
            P("mem", "lev", None, None),
            P("lev", None, None),
            P("mem", "lev", None),
            P(),
            P(),
            P("lev", None),
            P(),
            P("lev", None, None),
        ),
        out_specs=P("mem", "lev", None, None),
        check_vma=False,
    )
```

profile of v0, /device:TPU:0, one launch (start us, length us, event | category | flops | bytes accessed | tf_op | source)
XLA Modules:
  0.0 364.1 jit_solution(14634546903029611447)
XLA Ops:
  6.5 0.0 copy-start
  6.5 0.0 reduce-scatter.2.cloned.1.call-start
  6.5 0.9 reduce-window.9
  7.4 1.2 bitcast_subtract_fusion.starts
  8.6 60.5 %forward.1 = f32[8,16,6144]{2,1,0:T(8,128)} custom-call(s32[8]{0:T(128)} %bitcast_subtract_fusion.starts, f32[2048,256]{1,0:T(8,128)} %bitcast.26, f32[2048,256]{1,0:T(8,128)} %bitcast.23), custom_call_target="tpu_custom_call" | custom-call | tf_op jit(solution)/shard_map/forward/pallas_call | solution.py:210
  69.1 0.0 copy-start.1
  69.1 44.4 %all_to_all.10 = f32[8,16,6144]{2,1,0:T(8,128)S(1)} all-to-all(f32[8,16,6144]{2,1,0:T(8,128)} %forward.1), channel_id=1, replica_groups=mesh['mem'=16,'lev'=8] {'lev'}, dimensions={0} | all-to-all | bytes 6291456 | tf_op jit(solution)/shard_map/all_to_all | solution.py:220
  113.5 0.0 copy-done
  113.5 0.0 copy-done.1
  113.5 6.9 %convolution_multiply_fusion = f32[6144,128]{1,0:T(8,128)} fusion(f32[128,6144]{1,0:T(8,128)S(1)} %bitcast.21, f32[128,128]{1,0:T(8,128)S(1)} %copy-done, f32[1,6144,128]{2,1,0:T(8,128)S(1)} %copy-done.1), kind=kOutput, calls=%fused_computation | convolution fusion | flops 1208745984 | bytes 9502720 | tf_op jit(solution)/shard_map/ks,lk->sl/dot_general | solution.py:222
  120.4 0.0 reduce-scatter.2.cloned.1.call-update
  120.4 0.2 all-gather.2.cloned.1.call-start
  120.7 0.4 copy-done.3
  121.1 0.6 dynamic_slice.7
  122.9 0.6 dynamic_slice.6
  123.5 3.2 compare_select_fusion.slots
  126.7 4.0 %weights.1 = f32[384,128]{1,0:T(8,128)} custom-call(s32[1]{0:T(128)} %bitcast.6.base, s32[1,6144]{1,0:T(1,128)} %compare_select_fusion.slots, f32[6144,128]{1,0:T(8,128)} %bitcast.25), custom_call_target="tpu_custom_call" | custom-call | tf_op jit(solution)/shard_map/weights/pallas_call | solution.py:231
  130.7 65.4 %reduce-scatter.2.cloned.1.call-done = f32[384,128]{1,0:T(8,128)} async-done(((f32[6144,128]{1,0:T(8,128)}), f32[384,128]{1,0:T(8,128)}) %reduce-scatter.2.cloned.1.call-update) | async-done | bytes 196624 | tf_op jit(solution)/shard_map/reduce_scatter | solution.py:240
  196.1 1.7 mul.14
  197.8 0.0 all-gather.2.cloned.1.call-update
  197.8 50.4 %all-gather.2.cloned.1.call-done = f32[6144,128]{1,0:T(8,128)} async-done(((f32[384,128]{1,0:T(8,128)}), f32[6144,128]{1,0:T(8,128)}) %all-gather.2.cloned.1.call-update) | async-done | bytes 3145744 | tf_op jit(solution)/shard_map/all_gather | solution.py:241
  248.2 5.1 %fusion = f32[6144,128]{0,1:T(8,128)S(1)} fusion(f32[128,128]{1,0:T(8,128)S(1)} %copy-done, f32[6144,128]{1,0:T(8,128)} %all-gather.2.cloned.1.call-done, f32[1,6144,128]{2,1,0:T(8,128)S(1)} %copy-done.1), kind=kOutput, calls=%fused_computation.2 | convolution fusion | flops 1208745984 | bytes 9502720 | tf_op jit(solution)/shard_map/sl,lk->ks/dot_general | solution.py:242
  253.3 42.8 %all_to_all.11.blocks = f32[8,16,6144]{2,1,0:T(8,128)} all-to-all(f32[8,16,6144]{2,1,0:T(8,128)S(1)} %bitcast.22), channel_id=1, replica_groups=mesh['mem'=16,'lev'=8] {'lev'}, dimensions={0} | all-to-all | bytes 6291456 | tf_op jit(solution)/shard_map/all_to_all | solution.py:243
  296.1 61.2 %backward.1 = f32[2048,256]{1,0:T(8,128)} custom-call(s32[8]{0:T(128)} %bitcast_subtract_fusion.starts, f32[8,16,6144]{2,1,0:T(8,128)} %all_to_all.11.blocks, f32[2048,256]{1,0:T(8,128)} %bitcast.24), custom_call_target="tpu_custom_call" | custom-call | tf_op jit(solution)/shard_map/backward/pallas_call | solution.py:247
  (5 shorter events, 0.0 us)
Async XLA Ops:
  6.5 107.0 %copy-start = (f32[128,128]{1,0:T(8,128)S(1)}, f32[128,128]{1,0:T(8,128)}, u32[]{:S(2)}) copy-start(f32[128,128]{1,0:T(8,128)} %param.11) | copy-start | bytes 196612
  6.5 189.5 %reduce-scatter.2.cloned.1.call-start = ((), (), s32[]{:S(2)}) async-start(), calls=%async_computation.3 | async-start | bytes 3342336 | tf_op jit(solution)/shard_map/reduce_scatter | solution.py:240
  69.1 44.4 %copy-start.1 = (f32[1,6144,128]{2,1,0:T(8,128)S(1)}, f32[1,6144,128]{2,1,0:T(8,128)}, u32[]{:S(2)}) copy-start(f32[1,6144,128]{2,1,0:T(8,128)} %param.10) | copy-start | bytes 9437188
  120.4 0.7 copy-start.3
  120.4 2.5 copy-start.4
  120.4 3.1 copy-start.2
  120.4 127.8 %all-gather.2.cloned.1.call-start = ((), (), s32[]{:S(2)}) async-start(), calls=%async_computation.4 | async-start | bytes 3342336 | tf_op jit(solution)/shard_map/all_gather | solution.py:241
Sparse Core Ops, SparseCore 0:
  120.5 75.4 reduce-scatter.1
  198.5 49.6 all-gather.1
where the time goes:
time: 365 us; the launch traced here: 364 us
  Pallas kernels  126 us (35%)
  waiting for transfers between devices  116 us (32%)
  blocking collectives  87.2 us (24%)
  between operations  14.8 us (4%)
  matrix products  12 us (3%)
  other arithmetic  6.92 us (2%)
    reduce_scatter x1, waiting for transfers between devices, body(): lax.psum_scatter(perturb[0] * filtered, 'mem', scatter_dimension=0, tiled...  65.4 us
    pallas_call x1, Pallas kernels, body(): pl.pallas_call(functools.partial(backward_kernel, size_x), out_shape=jax....  61.2 us
    pallas_call x1, Pallas kernels, body(): pl.pallas_call(functools.partial(forward_kernel, size_x), out_shape=jax.S...  60.5 us
    all_gather x1, waiting for transfers between devices, body(): adjoint = lax.all_gather(part * weight, 'mem', axis=0, tiled=True)  50.4 us
    all_to_all x1, blocking collectives, body(): lax.all_to_all(pieces, 'lev', split_axis=0, concat_axis=0, tiled=True)  44.4 us
    all_to_all x1, blocking collectives, body(): lax.all_to_all(back.reshape(groups, levels, capacity), 'lev', split_axis=...  42.8 us
  transfers between devices with their start and end apart: 2, of which 2 were waited for; matrix products, arithmetic and copies ran while one was open for 1% of the time, Pallas kernels for 1%

commit v1 on v0

--- a/solution.py
+++ b/solution.py
@@ -7,8 +7,12 @@
 from jax.experimental.pallas import tpu as pltpu
 from jax.sharding import PartitionSpec as P
 
-STEPS = 4
+UNROLL = 16
 LANES = 128
+
+
+CHUNKS = 6
+MESH = pl.DeviceIdType.MESH
 
 
 def lane_index(shape):
@@ -32,7 +36,7 @@
         face_y[2 * i + 1] = jnp.where(lane == LANES - 1, 0.0, 0.5 * (k1 + r1))
         return n0, n1
 
-    lax.fori_loop(0, size_x, step, (load(0, 0), load(0, 1)))
+    lax.fori_loop(0, size_x, step, (load(0, 0), load(0, 1)), unroll=8)
 
 
 def diffuse_pass(load, store, face_x, face_y, size_x):
@@ -55,7 +59,7 @@
         store(i, 1, v1 + (x1 - above1) + (y1 - jnp.where(first, b0, b1)))
         return n0, n1, x0, x1
 
-    lax.fori_loop(0, size_x, step, (load(0, 0), load(0, 1), zero, zero), unroll=2)
+    lax.fori_loop(0, size_x, step, (load(0, 0), load(0, 1), zero, zero), unroll=UNROLL)
 
 
 def flat_access(ref):
@@ -86,7 +90,21 @@
 
 
 def forward_kernel(
-    size_x, starts, control_in, diff_in, pieces, face_x, face_y, one, two, control, diff, sems
+    size_x,
+    widths,
+    counts,
+    control_in,
+    diff_in,
+    raw,
+    pieces,
+    slots,
+    face_x,
+    face_y,
+    one,
+    two,
+    control,
+    diff,
+    sems,
 ):
     groups, levels, capacity = pieces.shape
     tiles = 2 * size_x
@@ -94,6 +112,9 @@
     control_copies = halves(control_in, control, sems.at[1])
     for copy in diff_copies + control_copies:
         copy.start()
+    position = lax.axis_index("lev")
+    order = lax.broadcasted_iota(jnp.int32, raw.shape, 0) * LANES + lane_index(raw.shape)
+    slots[...] = jnp.where(order < counts[position], lax.rem(raw[...], jnp.full(raw.shape, widths[position])), -1)
     for copy in diff_copies:
         copy.wait()
     make_faces(diff, face_x, face_y, size_x)
@@ -107,8 +128,9 @@
     diffuse_pass(load_two, store_one, face_x, face_y, size_x)
     diffuse_pass(load_one, store_two, face_x, face_y, size_x)
     lane = lane_index((levels, LANES))
+    end = jnp.int32(0)
     for group in range(groups):
-        start = starts[group]
+        start, end = end, end + widths[group]
         tile, shift = start // LANES, start % LANES
         keep = lane < LANES - shift
         back = (LANES - shift) % LANES
@@ -120,11 +142,11 @@
             return after
 
         begin = pltpu.roll(two[jnp.minimum(tile, tiles - 1)], back, 1)
-        lax.fori_loop(0, capacity // LANES, window, begin, unroll=4)
+        lax.fori_loop(0, capacity // LANES, window, begin, unroll=16)
 
 
 def backward_kernel(
-    size_x, starts, blocks, diff_in, out_to, face_x, face_y, one, two, out, diff, sems
+    size_x, widths, blocks, diff_in, out_to, face_x, face_y, one, two, out, diff, sems
 ):
     groups, levels, capacity = blocks.shape
     diff_copies = halves(diff_in, diff, sems.at[0])
@@ -134,8 +156,9 @@
         copy.wait()
     make_faces(diff, face_x, face_y, size_x)
     lane = lane_index((levels, LANES))
+    end = jnp.int32(0)
     for group in range(groups):
-        start = starts[group]
+        start, end = end, end + widths[group]
         tile, shift = start // LANES, start % LANES
         keep = lane >= shift
 
@@ -145,7 +168,7 @@
             one[tile + q] = jnp.where(keep, here, before)
             return here
 
-        tail = lax.fori_loop(0, capacity // LANES, place, one[tile], unroll=4)
+        tail = lax.fori_loop(0, capacity // LANES, place, one[tile], unroll=16)
         one[tile + capacity // LANES] = tail
     load_one, store_one = flat_access(one)
     load_two, store_two = flat_access(two)
@@ -170,18 +193,237 @@
     return high, low
 
 
-def weights_kernel(base, slots, rinv, out):
-    rows = out.shape[0]
-    total = rinv.shape[0]
-    block = 1024
-    acc = jnp.zeros((rows, 2 * LANES), jnp.float32)
-    here = base[0] + lax.broadcasted_iota(jnp.int32, (rows, block), 0)
-    for k in range(total // block):
-        high, low = split_two(rinv[k * block : (k + 1) * block, :])
-        chosen = (here == slots[:, k * block : (k + 1) * block]).astype(jnp.bfloat16)
-        both = jnp.concatenate([high, low], axis=1)
-        acc += jnp.dot(chosen, both, preferred_element_type=jnp.float32)
-    out[...] = acc[:, :LANES] + acc[:, LANES:]
+def middle_kernel(
+    chunks,
+    pieces,
+    perturb_in,
+    rinv_in,
+    vertical,
+    slots,
+    blocks,
+    column,
+    perturb,
+    rinv,
+    weight,
+    product,
+    from_core,
+    half,
+    from_z,
+    eighth,
+    from_x,
+    adjoint,
+    back,
+    load_sem,
+    in_send,
+    in_recv,
+    out_send,
+    out_recv,
+    core_send,
+    core_recv,
+    z_send,
+    z_recv,
+    x_send,
+    x_recv,
+):
+    groups, levels, capacity = pieces.shape
+    total = groups * levels
+    rows = capacity // chunks
+    mem, lev = lax.axis_index("mem"), lax.axis_index("lev")
+    z, x_hi, core = mem // 4, lax.rem(mem // 2, 2), lax.rem(mem, 2)
+    other_core = (mem + 1 - 2 * core, lev)
+    other_x = (mem + 2 - 4 * x_hi, lev)
+    others_z = [lax.rem(z + d, 4) for d in range(1, 4)]
+    across_z = [(there * 4 + x_hi * 2 + core, lev) for there in others_z]
+    others_lev = [lax.rem(lev + d, groups) for d in range(1, groups)]
+    across_lev = [(mem, there) for there in others_lev]
+    sources = [lax.rem(lev + groups - d, groups) for d in range(1, groups)]
+
+    loads = [
+        pltpu.make_async_copy(perturb_in, perturb, load_sem.at[0]),
+        pltpu.make_async_copy(rinv_in, rinv, load_sem.at[1]),
+        pltpu.make_async_copy(pieces.at[lev], column.at[lev], load_sem.at[2]),
+    ]
+    for copy in loads:
+        copy.start()
+
+    barrier = pltpu.get_barrier_semaphore()
+    everyone = [other_core, other_x] + across_z + across_lev
+    for device in everyone:
+        pl.semaphore_signal(barrier, 1, device_id=device, device_id_type=MESH)
+    pl.semaphore_wait(barrier, len(everyone))
+
+    pending = []
+
+    def send(source, target, send_sem, recv_sem, device):
+        copy = pltpu.make_async_remote_copy(
+            source, target, send_sem, recv_sem, device_id=device, device_id_type=MESH
+        )
+        copy.start()
+        pending.append(copy)
+
+    def arrived(target, recv_sem):
+        pltpu.make_async_remote_copy(
+            target, target, recv_sem, recv_sem, device_id=other_core, device_id_type=MESH
+        ).wait_recv()
+
+    def columns(k):
+        return pl.ds(k * rows, rows)
+
+    def enter(k):
+        for d in range(groups - 1):
+            send(
+                pieces.at[others_lev[d], :, columns(k)],
+                column.at[lev, :, columns(k)],
+                in_send.at[k, d],
+                in_recv.at[k, d],
+                across_lev[d],
+            )
+
+    def rows_at(k, *parts):
+        first, size = k * rows, rows
+        for index, count in parts:
+            size = size // count
+            first = first + index * size
+        return pl.ds(pl.multiple_of(first, 8), size)
+
+    def product_of(high, low, split, contract):
+        dims = (((1,), (contract,)), ((), ()))
+        v_high, v_low = split
+        dot = functools.partial(
+            lax.dot_general, dimension_numbers=dims, preferred_element_type=jnp.float32
+        )
+        return dot(high, v_high) + (dot(high, v_low) + dot(low, v_high))
+
+    enter(0)
+    enter(1)
+
+    owned = rows // 16
+    block = 512
+    first_row = core * (rows // 2) + z * (rows // 8) + x_hi * owned
+    here = jnp.concatenate(
+        [
+            first_row + k * rows + lax.broadcasted_iota(jnp.int32, (owned, LANES), 0)
+            for k in range(chunks)
+        ],
+        axis=0,
+    )
+    loads[1].wait()
+    weight[...] = jnp.zeros_like(weight)
+
+    def gather(b, _):
+        high, low = split_two(rinv[pl.ds(pl.multiple_of(b * block, block), block), :])
+        mine = slots[pl.ds(b * (block // LANES), block // LANES), :]
+        chosen = jnp.concatenate(
+            [
+                jnp.where(here == mine[q : q + 1, :], 1.0, 0.0).astype(jnp.bfloat16)
+                for q in range(block // LANES)
+            ],
+            axis=1,
+        )
+        dot = functools.partial(jnp.dot, preferred_element_type=jnp.float32)
+        weight[...] += dot(chosen, high) + dot(chosen, low)
+        return 0
+
+    lax.fori_loop(0, capacity // block, gather, 0)
+    split = split_two(vertical[...])
+    loads[0].wait()
+    loads[2].wait()
+    tile = 256
+
+    def contract_in(k):
+        for d in range(groups - 1):
+            arrived(column.at[sources[d], :, columns(k)], in_recv.at[k, d])
+        if k + 2 < chunks:
+            enter(k + 2)
+
+        def one(i, _):
+            at = pl.ds(pl.multiple_of(k * rows + i * tile, tile), tile)
+            high, low = split_two(column[:, :, at].reshape(total, tile).T)
+            product[at, :] = perturb[at, :] * product_of(high, low, split, 1)
+            return 0
+
+        lax.fori_loop(0, rows // tile, one, 0)
+        there = rows_at(k, (1 - core, 2))
+        send(product.at[there], from_core.at[k], core_send.at[0, k], core_recv.at[0, k], other_core)
+
+    def add_core(k):
+        arrived(from_core.at[k], core_recv.at[0, k])
+        half[k] = product[rows_at(k, (core, 2)), :] + from_core[k]
+        for d in range(3):
+            quarter = half.at[k, pl.ds(pl.multiple_of(others_z[d] * (rows // 8), 8), rows // 8)]
+            send(quarter, from_z.at[k, d], z_send.at[0, k, d], z_recv.at[0, k, d], across_z[d])
+
+    def add_z(k):
+        for d in range(3):
+            arrived(from_z.at[k, d], z_recv.at[0, k, d])
+        own = half[k, pl.ds(pl.multiple_of(z * (rows // 8), 8), rows // 8), :]
+        eighth[k] = (own + from_z[k, 0]) + (from_z[k, 1] + from_z[k, 2])
+        there = eighth.at[k, pl.ds(pl.multiple_of((1 - x_hi) * owned, 8), owned)]
+        send(there, from_x.at[k], x_send.at[0, k], x_recv.at[0, k], other_x)
+
+    def add_x(k):
+        arrived(from_x.at[k], x_recv.at[0, k])
+        own = eighth[k, pl.ds(pl.multiple_of(x_hi * owned, 8), owned), :]
+        at = rows_at(k, (core, 2), (z, 4), (x_hi, 2))
+        adjoint[at, :] = (own + from_x[k]) * weight[k * owned : (k + 1) * owned, :]
+        send(adjoint.at[at], adjoint.at[at], x_send.at[1, k], x_recv.at[1, k], other_x)
+
+    def give_z(k):
+        arrived(adjoint.at[rows_at(k, (core, 2), (z, 4), (1 - x_hi, 2))], x_recv.at[1, k])
+        at = rows_at(k, (core, 2), (z, 4))
+        for d in range(3):
+            send(adjoint.at[at], adjoint.at[at], z_send.at[1, k, d], z_recv.at[1, k, d], across_z[d])
+
+    def give_core(k):
+        for d in range(3):
+            there = lax.rem(z + 3 - d, 4)
+            arrived(adjoint.at[rows_at(k, (core, 2), (there, 4))], z_recv.at[1, k, d])
+        at = rows_at(k, (core, 2))
+        send(adjoint.at[at], adjoint.at[at], core_send.at[1, k], core_recv.at[1, k], other_core)
+
+    def contract_out(k):
+        arrived(adjoint.at[rows_at(k, (1 - core, 2))], core_recv.at[1, k])
+
+        def one(i, _):
+            at = pl.ds(pl.multiple_of(k * rows + i * tile, tile), tile)
+            high, low = split_two(perturb[at, :] * adjoint[at, :])
+            back[:, :, at] = product_of(high, low, split, 0).T.reshape(groups, levels, tile)
+            return 0
+
+        lax.fori_loop(0, rows // tile, one, 0)
+        for d in range(groups - 1):
+            send(
+                back.at[others_lev[d], :, columns(k)],
+                blocks.at[lev, :, columns(k)],
+                out_send.at[k, d],
+                out_recv.at[k, d],
+                across_lev[d],
+            )
+        pltpu.make_async_copy(
+            back.at[lev, :, columns(k)], blocks.at[lev, :, columns(k)], load_sem.at[3 + k]
+        ).start()
+
+    for step in range(chunks + 3):
+        for stage, lag in (
+            (contract_in, 0),
+            (add_z, 1),
+            (give_z, 2),
+            (add_core, 0),
+            (add_x, 1),
+            (give_core, 2),
+            (contract_out, 3),
+        ):
+            if 0 <= step - lag < chunks:
+                stage(step - lag)
+
+    for k in range(chunks):
+        for d in range(groups - 1):
+            arrived(blocks.at[sources[d], :, columns(k)], out_recv.at[k, d])
+        pltpu.make_async_copy(
+            back.at[lev, :, columns(k)], blocks.at[lev, :, columns(k)], load_sem.at[3 + k]
+        ).wait()
+    for copy in pending:
+        copy.wait_send()
 
 
 SMEM = pl.BlockSpec(memory_space=pltpu.SMEM)
@@ -195,64 +437,84 @@
     capacity = perturb.shape[1]
     groups = sub_widths.shape[0]
     tiles = 2 * size_x
-    highest = lax.Precision.HIGHEST
-    starts = jnp.cumsum(sub_widths) - sub_widths
+    f32 = jnp.float32
     diff = diffusivity.reshape(levels * size_x, size_y)
     scratch = [
-        pltpu.VMEM((tiles, levels, LANES), jnp.float32),
-        pltpu.VMEM((tiles, levels, LANES), jnp.float32),
-        pltpu.VMEM((tiles + capacity // LANES + 1, levels, LANES), jnp.float32),
-        pltpu.VMEM((tiles, levels, LANES), jnp.float32),
-        pltpu.VMEM((2, levels * size_x, LANES), jnp.float32),
-        pltpu.VMEM((2, levels * size_x, LANES), jnp.float32),
+        pltpu.VMEM((tiles, levels, LANES), f32),
+        pltpu.VMEM((tiles, levels, LANES), f32),
+        pltpu.VMEM((tiles + capacity // LANES + 1, levels, LANES), f32),
+        pltpu.VMEM((tiles, levels, LANES), f32),
+        pltpu.VMEM((2, levels * size_x, LANES), f32),
+        pltpu.VMEM((2, levels * size_x, LANES), f32),
         pltpu.SemaphoreType.DMA((2, 2)),
     ]
-    pieces = pl.pallas_call(
+    lines = capacity // LANES
+    pieces, slots = pl.pallas_call(
         functools.partial(forward_kernel, size_x),
-        out_shape=jax.ShapeDtypeStruct((groups, levels, capacity), jnp.float32),
-        in_specs=[SMEM, ANY, ANY],
-        out_specs=VMEM,
+        out_shape=(
+            jax.ShapeDtypeStruct((groups, levels, capacity), f32),
+            jax.ShapeDtypeStruct((lines, LANES), jnp.int32),
+        ),
+        in_specs=[SMEM, SMEM, ANY, ANY, VMEM],
+        out_specs=(VMEM, VMEM),
         scratch_shapes=scratch,
         compiler_params=pltpu.CompilerParams(vmem_limit_bytes=LIMIT),
         name="forward",
-    )(starts, control.reshape(levels * size_x, size_y), diff)
-
-    column_form = lax.all_to_all(pieces, "lev", split_axis=0, concat_axis=0, tiled=True)
-    column_form = column_form.reshape(groups * levels, capacity)
-    filtered = jnp.einsum("ks,lk->sl", column_form, vertical_filter, precision=highest)
-
-    position = lax.axis_index("lev")
-    width = sub_widths[position]
-    slots = obs_raw % width
-    live = jnp.arange(obs_raw.shape[1], dtype=jnp.int32)[None] < obs_counts[position]
-    slots = jnp.where(live, slots, -1)
-    owned = capacity // lax.axis_size("mem")
-    base = (lax.axis_index("mem") * owned).astype(jnp.int32).reshape(1)
-    weight = pl.pallas_call(
-        weights_kernel,
-        out_shape=jax.ShapeDtypeStruct((owned, groups * levels), jnp.float32),
-        in_specs=[SMEM, VMEM, VMEM],
+    )(
+        sub_widths,
+        obs_counts,
+        control.reshape(levels * size_x, size_y),
+        diff,
+        obs_raw.reshape(lines, LANES),
+    )
+
+    rows = capacity // CHUNKS
+    dma = pltpu.SemaphoreType.DMA
+    blocks = pl.pallas_call(
+        functools.partial(middle_kernel, CHUNKS),
+        out_shape=jax.ShapeDtypeStruct((groups, levels, capacity), f32),
+        in_specs=[ANY, ANY, ANY, VMEM, VMEM],
         out_specs=VMEM,
-        compiler_params=pltpu.CompilerParams(vmem_limit_bytes=LIMIT),
-        name="weights",
-    )(base, slots, obs_rinv[0])
-
-    part = lax.psum_scatter(perturb[0] * filtered, "mem", scatter_dimension=0, tiled=True)
-    adjoint = lax.all_gather(part * weight, "mem", axis=0, tiled=True)
-    back = jnp.einsum("sl,lk->ks", perturb[0] * adjoint, vertical_filter, precision=highest)
-    blocks = lax.all_to_all(
-        back.reshape(groups, levels, capacity), "lev", split_axis=0, concat_axis=0, tiled=True
-    )
+        scratch_shapes=[
+            pltpu.VMEM((groups, levels, capacity), f32),
+            pltpu.VMEM((capacity, LANES), f32),
+            pltpu.VMEM((capacity, LANES), f32),
+            pltpu.VMEM((capacity // 16, LANES), f32),
+            pltpu.VMEM((capacity, LANES), f32),
+            pltpu.VMEM((CHUNKS, rows // 2, LANES), f32),
+            pltpu.VMEM((CHUNKS, rows // 2, LANES), f32),
+            pltpu.VMEM((CHUNKS, 3, rows // 8, LANES), f32),
+            pltpu.VMEM((CHUNKS, rows // 8, LANES), f32),
+            pltpu.VMEM((CHUNKS, rows // 16, LANES), f32),
+            pltpu.VMEM((capacity, LANES), f32),
+            pltpu.VMEM((groups, levels, capacity), f32),
+            dma((3 + CHUNKS,)),
+            dma((CHUNKS, groups - 1)),
+            dma((CHUNKS, groups - 1)),
+            dma((CHUNKS, groups - 1)),
+            dma((CHUNKS, groups - 1)),
+            dma((2, CHUNKS)),
+            dma((2, CHUNKS)),
+            dma((2, CHUNKS, 3)),
+            dma((2, CHUNKS, 3)),
+            dma((2, CHUNKS)),
+            dma((2, CHUNKS)),
+        ],
+        compiler_params=pltpu.CompilerParams(
+            vmem_limit_bytes=LIMIT, collective_id=0, has_side_effects=True
+        ),
+        name="middle",
+    )(pieces, perturb[0], obs_rinv[0], vertical_filter, slots)
 
     out = pl.pallas_call(
         functools.partial(backward_kernel, size_x),
-        out_shape=jax.ShapeDtypeStruct((levels * size_x, size_y), jnp.float32),
+        out_shape=jax.ShapeDtypeStruct((levels * size_x, size_y), f32),
         in_specs=[SMEM, VMEM, ANY],
         out_specs=ANY,
         scratch_shapes=scratch,
         compiler_params=pltpu.CompilerParams(vmem_limit_bytes=LIMIT),
         name="backward",
-    )(starts, blocks, diff)
+    )(sub_widths, blocks, diff)
     return out.reshape(control.shape)
 
 

time: 365 us -> 143 us (0.39)
  waiting for transfers between devices: 116 us -> 0 us
  blocking collectives: 87.2 us -> 0 us
  Pallas kernels: 126 us -> 143 us
  between operations: 14.8 us -> 0.02 us
  matrix products: 12 us -> 0 us
  other arithmetic: 6.92 us -> 0 us
    all_to_all x2 -> x0, blocking collectives: 87.2 us -> none  [the longest x1 44.4 us: body(): lax.all_to_all(pieces, 'lev', split_axis=0, concat_axis=0, tiled=True)]
    reduce_scatter x1 -> x0, waiting for transfers between devices: 65.4 us -> none  [body(): lax.psum_scatter(perturb[0] * filtered, 'mem', scatter_dimension=0, tiled...]
    pallas_call x2, Pallas kernels: 64.5 us -> 123 us  [the longest x1 103 us: body(): pl.pallas_call(functools.partial(middle_kernel, CHUNKS), out_shape=jax.Sh...]
    all_gather x1 -> x0, waiting for transfers between devices: 50.4 us -> none  [body(): adjoint = lax.all_gather(part * weight, 'mem', axis=0, tiled=True)]
    pallas_call x1, Pallas kernels: 61.2 us -> 20.4 us  [body(): pl.pallas_call(functools.partial(backward_kernel, size_x), out_shape=jax....]
    dot_general x2 -> x0, matrix products: 12 us -> none  [the longest x1 6.88 us: body(): jnp.einsum('ks,lk->sl', column_form, vertical_filter, precision=highest)]
  transfers between devices with their start and end apart: 2 -> 0, of which waited for: 2 -> 0; matrix products, arithmetic and copies ran while one was open for 1% -> 0% of each run, Pallas kernels for 1% -> 0%
where the time goes in v1:
time: 143 us
  Pallas kernels  143 us (100%)
    pallas_call x1, Pallas kernels, body(): pl.pallas_call(functools.partial(middle_kernel, CHUNKS), out_shape=jax.Sh...  103 us
    pallas_call x1, Pallas kernels, body(): pl.pallas_call(functools.partial(backward_kernel, size_x), out_shape=jax....  20.4 us
    pallas_call x1, Pallas kernels, body(): pl.pallas_call(functools.partial(forward_kernel, size_x), out_shape=(jax....  20 us

profile of v1, /device:TPU:0, one launch (start us, length us, event | category | flops | bytes accessed | tf_op | source)
XLA Modules:
  0.0 143.1 jit_solution(1162167864273725581)
XLA Ops:
  0.0 20.0 %forward.1 = (f32[8,16,6144]{2,1,0:T(8,128)}, s32[48,128]{1,0:T(8,128)}) custom-call(s32[8]{0:T(128)} %widths.3, s32[8]{0:T(128)} %counts.1, f32[2048,256]{1,0:T(8,128)} %bitcast.10, f32[2048,256]{1,0:T(8,128)} %bitcast.6, s32[48,128]{1,0:T(8,128)} %bitcast.11), custom_call_target="tpu_custom_call" | custom-call | tf_op jit(solution)/shard_map/forward/pallas_call | solution.py:452
  20.0 102.7 %middle.1.blocks = f32[8,16,6144]{2,1,0:T(8,128)} custom-call(f32[8,16,6144]{2,1,0:T(8,128)} %get-tuple-element.7.pieces, f32[6144,128]{1,0:T(8,128)} %bitcast.8, f32[6144,128]{1,0:T(8,128)} %bitcast.9, f32[128,128]{1,0:T(8,128)} %vertical.1, s32[48,128]{1,0:T(8,128)} %get-tuple-element.8.slots), custom_call_target="tpu_custom_call" | custom-call | tf_op jit(solution)/shard_map/middle/pallas_call | solution.py:473
  122.6 20.4 %backward.1 = f32[2048,256]{1,0:T(8,128)} custom-call(s32[8]{0:T(128)} %widths.3, f32[8,16,6144]{2,1,0:T(8,128)} %middle.1.blocks, f32[2048,256]{1,0:T(8,128)} %bitcast.7), custom_call_target="tpu_custom_call" | custom-call | tf_op jit(solution)/shard_map/backward/pallas_call | solution.py:509

commit v2 on v1

--- a/solution.py
+++ b/solution.py
@@ -7,11 +7,15 @@
 from jax.experimental.pallas import tpu as pltpu
 from jax.sharding import PartitionSpec as P
 
-UNROLL = 16
+UNROLL = 32
+WINDOW = 48
+SUB = 8
 LANES = 128
 
 
-CHUNKS = 6
+CHUNKS = 8
+PACE = 2
+SCHED = (("F", 0), ("A", 0), ("B", 1), ("C", 2), ("D", 3), ("E", 4), ("G", 5))
 MESH = pl.DeviceIdType.MESH
 
 
@@ -19,171 +23,158 @@
     return lax.broadcasted_iota(jnp.int32, shape, len(shape) - 1)
 
 
-def make_faces(diff_ref, face_x, face_y, size_x):
-    levels = face_x.shape[1]
-    lane = lane_index((levels, LANES))
-    load, _ = rows_access(diff_ref, size_x, levels)
+def make_faces(diff, face_x, face_y, size_x, part):
+    lane = lane_index((SUB, LANES))
+    last = lane == LANES - 1
+    at = pl.ds(part * SUB, SUB)
 
     def step(i, here):
         k0, k1 = here
-        after = jnp.minimum(i + 1, size_x - 1)
-        n0, n1 = load(after, 0), load(after, 1)
-        inner = jnp.where(i < size_x - 1, 0.5, 0.0)
-        face_x[2 * i] = inner * (k0 + n0)
-        face_x[2 * i + 1] = inner * (k1 + n1)
+        n0, n1 = diff[i + 1, 0, at, :], diff[i + 1, 1, at, :]
+        face_x[i, 0, at, :] = 0.5 * (k0 + n0)
+        face_x[i, 1, at, :] = 0.5 * (k1 + n1)
         r0, r1 = pltpu.roll(k0, LANES - 1, 1), pltpu.roll(k1, LANES - 1, 1)
-        face_y[2 * i] = 0.5 * (k0 + jnp.where(lane == LANES - 1, r1, r0))
-        face_y[2 * i + 1] = jnp.where(lane == LANES - 1, 0.0, 0.5 * (k1 + r1))
+        face_y[i, 0, at, :] = 0.5 * (k0 + jnp.where(last, r1, r0))
+        face_y[i, 1, at, :] = jnp.where(last, 0.0, 0.5 * (k1 + r1))
         return n0, n1
 
-    lax.fori_loop(0, size_x, step, (load(0, 0), load(0, 1)), unroll=8)
-
-
-def diffuse_pass(load, store, face_x, face_y, size_x):
-    levels = face_x.shape[1]
-    lane = lane_index((levels, LANES))
+    lax.fori_loop(0, size_x, step, (diff[0, 0, at, :], diff[0, 1, at, :]), unroll=UNROLL)
+    face_x[size_x - 1, :, at, :] = jnp.zeros((2, SUB, LANES), jnp.float32)
+
+
+def clear_edge(ref, first):
+    ref[first:] = jnp.zeros((ref.shape[0] - first, *ref.shape[1:]), jnp.float32)
+
+
+def row_of(ref, i, half):
+    return (2 * i + half,) if len(ref.shape) == 3 else (i, half)
+
+
+def diffuse_pass(source, target, face_x, face_y, size_x, part):
+    lane = lane_index((SUB, LANES))
     last, first = lane == LANES - 1, lane == 0
-    zero = jnp.zeros((levels, LANES), jnp.float32)
+    zero = jnp.zeros((SUB, LANES), jnp.float32)
+    at = pl.ds(part * SUB, SUB)
 
     def step(i, carry):
         v0, v1, above0, above1 = carry
-        after = jnp.minimum(i + 1, size_x - 1)
-        n0, n1 = load(after, 0), load(after, 1)
-        x0 = face_x[2 * i] * (n0 - v0)
-        x1 = face_x[2 * i + 1] * (n1 - v1)
+        n0, n1 = (source[*row_of(source, i + 1, half), at, :] for half in range(2))
+        x0 = face_x[i, 0, at, :] * (n0 - v0)
+        x1 = face_x[i, 1, at, :] * (n1 - v1)
         r0, r1 = pltpu.roll(v0, LANES - 1, 1), pltpu.roll(v1, LANES - 1, 1)
-        y0 = face_y[2 * i] * (jnp.where(last, r1, r0) - v0)
-        y1 = face_y[2 * i + 1] * (r1 - v1)
+        y0 = face_y[i, 0, at, :] * (jnp.where(last, r1, r0) - v0)
+        y1 = face_y[i, 1, at, :] * (r1 - v1)
         b0, b1 = pltpu.roll(y0, 1, 1), pltpu.roll(y1, 1, 1)
-        store(i, 0, v0 + (x0 - above0) + (y0 - jnp.where(first, b1, b0)))
-        store(i, 1, v1 + (x1 - above1) + (y1 - jnp.where(first, b0, b1)))
+        target[*row_of(target, i, 0), at, :] = v0 + (x0 - above0) + (y0 - jnp.where(first, b1, b0))
+        target[*row_of(target, i, 1), at, :] = v1 + (x1 - above1) + (y1 - jnp.where(first, b0, b1))
         return n0, n1, x0, x1
 
-    lax.fori_loop(0, size_x, step, (load(0, 0), load(0, 1), zero, zero), unroll=UNROLL)
-
-
-def flat_access(ref):
-    def load(i, half):
-        return ref[2 * i + half]
-
-    def store(i, half, value):
-        ref[2 * i + half] = value
-
-    return load, store
-
-
-def rows_access(ref, size_x, levels):
-    def load(i, half):
-        return ref[half, pl.ds(i, levels, stride=size_x), :]
-
-    def store(i, half, value):
-        ref[half, pl.ds(i, levels, stride=size_x), :] = value
-
-    return load, store
-
-
-def halves(array, scratch, sems):
-    return [
-        pltpu.make_async_copy(array.at[:, pl.ds(h * LANES, LANES)], scratch.at[h], sems.at[h])
-        for h in range(2)
-    ]
+    begin = (*(source[*row_of(source, 0, half), at, :] for half in range(2)), zero, zero)
+    lax.fori_loop(0, size_x, step, begin, unroll=UNROLL)
+
+
+def by_level(grid, field, sems, part, out=False):
+    size_x = grid.shape[1]
+    copies = []
+    for level in range(part * SUB, (part + 1) * SUB):
+        for half in range(2):
+            there = grid.at[level, :, pl.ds(half * LANES, LANES)]
+            here = field.at[pl.ds(0, size_x), half, level, :]
+            pair = (here, there) if out else (there, here)
+            copies.append(pltpu.make_async_copy(*pair, sems.at[level, half]))
+    return copies
 
 
 def forward_kernel(
-    size_x,
-    widths,
-    counts,
-    control_in,
-    diff_in,
-    raw,
-    pieces,
-    slots,
-    face_x,
-    face_y,
-    one,
-    two,
-    control,
-    diff,
-    sems,
+    widths, counts, control_in, diff_in, raw, pieces, slots, face_x, face_y, control, one, two, diff, sems
 ):
     groups, levels, capacity = pieces.shape
+    size_x = control_in.shape[1]
     tiles = 2 * size_x
-    diff_copies = halves(diff_in, diff, sems.at[0])
-    control_copies = halves(control_in, control, sems.at[1])
-    for copy in diff_copies + control_copies:
-        copy.start()
+    parts = levels // SUB
+    diff_copies = [by_level(diff_in, diff, sems.at[0], part) for part in range(parts)]
+    control_copies = [by_level(control_in, control, sems.at[1], part) for part in range(parts)]
+    for part in range(parts):
+        for copy in diff_copies[part] + control_copies[part]:
+            copy.start()
+    clear_edge(control, size_x)
+    clear_edge(one, tiles)
+    clear_edge(two, tiles)
     position = lax.axis_index("lev")
     order = lax.broadcasted_iota(jnp.int32, raw.shape, 0) * LANES + lane_index(raw.shape)
-    slots[...] = jnp.where(order < counts[position], lax.rem(raw[...], jnp.full(raw.shape, widths[position])), -1)
-    for copy in diff_copies:
-        copy.wait()
-    make_faces(diff, face_x, face_y, size_x)
-    for copy in control_copies:
-        copy.wait()
-    load_in, _ = rows_access(control, size_x, levels)
-    load_one, store_one = flat_access(one)
-    load_two, store_two = flat_access(two)
-    diffuse_pass(load_in, store_one, face_x, face_y, size_x)
-    diffuse_pass(load_one, store_two, face_x, face_y, size_x)
-    diffuse_pass(load_two, store_one, face_x, face_y, size_x)
-    diffuse_pass(load_one, store_two, face_x, face_y, size_x)
-    lane = lane_index((levels, LANES))
-    end = jnp.int32(0)
-    for group in range(groups):
-        start, end = end, end + widths[group]
-        tile, shift = start // LANES, start % LANES
-        keep = lane < LANES - shift
-        back = (LANES - shift) % LANES
-
-        def window(q, here):
-            after = pltpu.roll(two[jnp.minimum(tile + q + 1, tiles - 1)], back, 1)
-            at = pl.multiple_of(q * LANES, LANES)
-            pieces[group, :, pl.ds(at, LANES)] = jnp.where(keep, here, after)
-            return after
-
-        begin = pltpu.roll(two[jnp.minimum(tile, tiles - 1)], back, 1)
-        lax.fori_loop(0, capacity // LANES, window, begin, unroll=16)
+    code = lax.rem(raw[...], jnp.full(raw.shape, widths[position]))
+    slots[...] = jnp.where(order < counts[position], code, -1)
+    lane = lane_index((SUB, LANES))
+    for part in range(parts):
+        at = pl.ds(part * SUB, SUB)
+        for copy in diff_copies[part]:
+            copy.wait()
+        make_faces(diff, face_x, face_y, size_x, part)
+        for copy in control_copies[part]:
+            copy.wait()
+        for source, target in ((control, two), (two, one), (one, two), (two, one)):
+            diffuse_pass(source, target, face_x, face_y, size_x, part)
+        end = jnp.int32(0)
+        for group in range(groups):
+            start, end = end, end + widths[group]
+            tile, shift = start // LANES, start % LANES
+            keep = lane < LANES - shift
+            back = (LANES - shift) % LANES
+
+            def rolled(t):
+                return pltpu.roll(one[t, at, :], back, 1)
+
+            def window(q, here):
+                after = rolled(tile + q + 1)
+                to = pl.multiple_of(q * LANES, LANES)
+                pieces[group, at, pl.ds(to, LANES)] = jnp.where(keep, here, after)
+                return after
+
+            lax.fori_loop(0, capacity // LANES, window, rolled(tile), unroll=WINDOW)
 
 
 def backward_kernel(
-    size_x, widths, blocks, diff_in, out_to, face_x, face_y, one, two, out, diff, sems
+    widths, blocks, diff_in, out_to, face_x, face_y, one, two, result, diff, sems
 ):
     groups, levels, capacity = blocks.shape
-    diff_copies = halves(diff_in, diff, sems.at[0])
-    for copy in diff_copies:
-        copy.start()
-    for copy in diff_copies:
-        copy.wait()
-    make_faces(diff, face_x, face_y, size_x)
-    lane = lane_index((levels, LANES))
-    end = jnp.int32(0)
-    for group in range(groups):
-        start, end = end, end + widths[group]
-        tile, shift = start // LANES, start % LANES
-        keep = lane >= shift
-
-        def place(q, before):
-            at = pl.multiple_of(q * LANES, LANES)
-            here = pltpu.roll(blocks[group, :, pl.ds(at, LANES)], shift, 1)
-            one[tile + q] = jnp.where(keep, here, before)
-            return here
-
-        tail = lax.fori_loop(0, capacity // LANES, place, one[tile], unroll=16)
-        one[tile + capacity // LANES] = tail
-    load_one, store_one = flat_access(one)
-    load_two, store_two = flat_access(two)
-    _, store_out = rows_access(out, size_x, levels)
-    diffuse_pass(load_one, store_two, face_x, face_y, size_x)
-    diffuse_pass(load_two, store_one, face_x, face_y, size_x)
-    diffuse_pass(load_one, store_two, face_x, face_y, size_x)
-    diffuse_pass(load_two, store_out, face_x, face_y, size_x)
-    copies = [
-        pltpu.make_async_copy(out.at[h], out_to.at[:, pl.ds(h * LANES, LANES)], sems.at[1, h])
-        for h in range(2)
-    ]
-    for copy in copies:
-        copy.start()
-    for copy in copies:
+    size_x = diff_in.shape[1]
+    parts = levels // SUB
+    diff_copies = [by_level(diff_in, diff, sems.at[0], part) for part in range(parts)]
+    for part in range(parts):
+        for copy in diff_copies[part]:
+            copy.start()
+    lane = lane_index((SUB, LANES))
+    for part in range(parts):
+        at = pl.ds(part * SUB, SUB)
+        end = jnp.int32(0)
+        for group in range(groups):
+            start, end = end, end + widths[group]
+            tile, shift = start // LANES, start % LANES
+            keep = lane >= shift
+
+            def place(q, before):
+                to = pl.multiple_of(q * LANES, LANES)
+                here = pltpu.roll(blocks[group, at, pl.ds(to, LANES)], shift, 1)
+                one[tile + q, at, :] = jnp.where(keep, here, before)
+                return here
+
+            begin = one[tile, at, :]
+            tail = lax.fori_loop(0, capacity // LANES, place, begin, unroll=WINDOW)
+            one[tile + capacity // LANES, at, :] = tail
+    clear_edge(one, 2 * size_x)
+    clear_edge(two, 2 * size_x)
+    outs = []
+    for part in range(parts):
+        for copy in diff_copies[part]:
+            copy.wait()
+        make_faces(diff, face_x, face_y, size_x, part)
+        for source, target in ((one, two), (two, one), (one, two), (two, result)):
+            diffuse_pass(source, target, face_x, face_y, size_x, part)
+        copies = by_level(out_to, result, sems.at[1], part, out=True)
+        for copy in copies:
+            copy.start()
+        outs += copies
+    for copy in outs:
         copy.wait()
 
 
@@ -294,8 +285,8 @@
         )
         return dot(high, v_high) + (dot(high, v_low) + dot(low, v_high))
 
-    enter(0)
-    enter(1)
+    for k in range(min(PACE, chunks)):
+        enter(k)
 
     owned = rows // 16
     block = 512
@@ -333,8 +324,8 @@
     def contract_in(k):
         for d in range(groups - 1):
             arrived(column.at[sources[d], :, columns(k)], in_recv.at[k, d])
-        if k + 2 < chunks:
-            enter(k + 2)
+        if k + PACE < chunks:
+            enter(k + PACE)
 
         def one(i, _):
             at = pl.ds(pl.multiple_of(k * rows + i * tile, tile), tile)
@@ -403,18 +394,11 @@
             back.at[lev, :, columns(k)], blocks.at[lev, :, columns(k)], load_sem.at[3 + k]
         ).start()
 
-    for step in range(chunks + 3):
-        for stage, lag in (
-            (contract_in, 0),
-            (add_z, 1),
-            (give_z, 2),
-            (add_core, 0),
-            (add_x, 1),
-            (give_core, 2),
-            (contract_out, 3),
-        ):
+    stages = dict(F=contract_in, A=add_core, B=add_z, C=add_x, D=give_z, E=give_core, G=contract_out)
+    for step in range(chunks + 6):
+        for stage, lag in SCHED:
             if 0 <= step - lag < chunks:
-                stage(step - lag)
+                stages[stage](step - lag)
 
     for k in range(chunks):
         for d in range(groups - 1):
@@ -436,40 +420,25 @@
     members, levels, size_x, size_y = control.shape
     capacity = perturb.shape[1]
     groups = sub_widths.shape[0]
-    tiles = 2 * size_x
     f32 = jnp.float32
-    diff = diffusivity.reshape(levels * size_x, size_y)
-    scratch = [
-        pltpu.VMEM((tiles, levels, LANES), f32),
-        pltpu.VMEM((tiles, levels, LANES), f32),
-        pltpu.VMEM((tiles + capacity // LANES + 1, levels, LANES), f32),
-        pltpu.VMEM((tiles, levels, LANES), f32),
-        pltpu.VMEM((2, levels * size_x, LANES), f32),
-        pltpu.VMEM((2, levels * size_x, LANES), f32),
-        pltpu.SemaphoreType.DMA((2, 2)),
-    ]
+    field = pltpu.VMEM((size_x + 1, 2, levels, LANES), f32)
+    dma = pltpu.SemaphoreType.DMA
     lines = capacity // LANES
+    wide = pltpu.VMEM((2 * size_x + lines + 2, levels, LANES), f32)
     pieces, slots = pl.pallas_call(
-        functools.partial(forward_kernel, size_x),
+        forward_kernel,
         out_shape=(
             jax.ShapeDtypeStruct((groups, levels, capacity), f32),
             jax.ShapeDtypeStruct((lines, LANES), jnp.int32),
         ),
         in_specs=[SMEM, SMEM, ANY, ANY, VMEM],
         out_specs=(VMEM, VMEM),
-        scratch_shapes=scratch,
+        scratch_shapes=[field, field, field, wide, wide, field, dma((2, levels, 2))],
         compiler_params=pltpu.CompilerParams(vmem_limit_bytes=LIMIT),
         name="forward",
-    )(
-        sub_widths,
-        obs_counts,
-        control.reshape(levels * size_x, size_y),
-        diff,
-        obs_raw.reshape(lines, LANES),
-    )
+    )(sub_widths, obs_counts, control[0], diffusivity, obs_raw.reshape(lines, LANES))
 
     rows = capacity // CHUNKS
-    dma = pltpu.SemaphoreType.DMA
     blocks = pl.pallas_call(
         functools.partial(middle_kernel, CHUNKS),
         out_shape=jax.ShapeDtypeStruct((groups, levels, capacity), f32),
@@ -507,14 +476,14 @@
     )(pieces, perturb[0], obs_rinv[0], vertical_filter, slots)
 
     out = pl.pallas_call(
-        functools.partial(backward_kernel, size_x),
-        out_shape=jax.ShapeDtypeStruct((levels * size_x, size_y), f32),
+        backward_kernel,
+        out_shape=jax.ShapeDtypeStruct((levels, size_x, size_y), f32),
         in_specs=[SMEM, VMEM, ANY],
         out_specs=ANY,
-        scratch_shapes=scratch,
+        scratch_shapes=[field, field, wide, wide, field, field, dma((2, levels, 2))],
         compiler_params=pltpu.CompilerParams(vmem_limit_bytes=LIMIT),
         name="backward",
-    )(sub_widths, blocks, diff)
+    )(sub_widths, blocks, diffusivity)
     return out.reshape(control.shape)
 
 

time: 143 us -> 120 us (0.84)
  Pallas kernels: 143 us -> 120 us
    pallas_call x1, Pallas kernels: 103 us -> 90.8 us  [body(): pl.pallas_call(functools.partial(middle_kernel, CHUNKS), out_shape=jax.Sh...]
    pallas_call x2, Pallas kernels: 40.4 us -> 29.1 us  [the longest x1 14.8 us: body(): pl.pallas_call(forward_kernel, out_shape=(jax.ShapeDtypeStruct((groups, l...]
where the time goes in v2:
time: 120 us
  Pallas kernels  120 us (100%)
    pallas_call x1, Pallas kernels, body(): pl.pallas_call(functools.partial(middle_kernel, CHUNKS), out_shape=jax.Sh...  90.8 us
    pallas_call x1, Pallas kernels, body(): pl.pallas_call(forward_kernel, out_shape=(jax.ShapeDtypeStruct((groups, l...  14.8 us
    pallas_call x1, Pallas kernels, body(): pl.pallas_call(backward_kernel, out_shape=jax.ShapeDtypeStruct((levels, s...  14.3 us

profile of v2, /device:TPU:0, one launch (start us, length us, event | category | flops | bytes accessed | tf_op | source)
XLA Modules:
  0.0 119.9 jit_solution(14679894080846106270)
XLA Ops:
  0.0 14.8 %forward.1 = (f32[8,16,6144]{2,1,0:T(8,128)}, s32[48,128]{1,0:T(8,128)}) custom-call(s32[8]{0:T(128)} %widths.3, s32[8]{0:T(128)} %counts.1, f32[16,128,256]{2,1,0:T(8,128)} %bitcast.7, f32[16,128,256]{2,1,0:T(8,128)} %diff_in.3, s32[48,128]{1,0:T(8,128)} %bitcast.8), custom_call_target="tpu_custom_call" | custom-call | tf_op jit(solution)/shard_map/forward/pallas_call | solution.py:428
  14.8 90.8 %middle.1.blocks = f32[8,16,6144]{2,1,0:T(8,128)} custom-call(f32[8,16,6144]{2,1,0:T(8,128)} %get-tuple-element.7.pieces, f32[6144,128]{1,0:T(8,128)} %bitcast.5, f32[6144,128]{1,0:T(8,128)} %bitcast.6, f32[128,128]{1,0:T(8,128)} %vertical.1, s32[48,128]{1,0:T(8,128)} %get-tuple-element.8.slots), custom_call_target="tpu_custom_call" | custom-call | tf_op jit(solution)/shard_map/middle/pallas_call | solution.py:442
  105.6 14.3 %backward.1 = f32[16,128,256]{2,1,0:T(8,128)} custom-call(s32[8]{0:T(128)} %widths.3, f32[8,16,6144]{2,1,0:T(8,128)} %middle.1.blocks, f32[16,128,256]{2,1,0:T(8,128)} %diff_in.3), custom_call_target="tpu_custom_call" | custom-call | tf_op jit(solution)/shard_map/backward/pallas_call | solution.py:478

commit v3 on v2

--- a/solution.py
+++ b/solution.py
@@ -42,8 +42,9 @@
     face_x[size_x - 1, :, at, :] = jnp.zeros((2, SUB, LANES), jnp.float32)
 
 
-def clear_edge(ref, first):
-    ref[first:] = jnp.zeros((ref.shape[0] - first, *ref.shape[1:]), jnp.float32)
+def clear_edge(ref, first, part):
+    shape = (ref.shape[0] - first, *ref.shape[1:-2], SUB, LANES)
+    ref[first:, ..., pl.ds(part * SUB, SUB), :] = jnp.zeros(shape, jnp.float32)
 
 
 def row_of(ref, i, half):
@@ -85,28 +86,151 @@
     return copies
 
 
-def forward_kernel(
-    widths, counts, control_in, diff_in, raw, pieces, slots, face_x, face_y, control, one, two, diff, sems
+def backward_kernel(
+    widths, blocks_in, faces_in, out_to, faces, blocks, one, two, result, sems, out_sems
+):
+    groups, levels, capacity = blocks.shape
+    size_x = out_to.shape[1]
+    parts = levels // SUB
+    face_x, face_y = faces.at[0], faces.at[1]
+    loads = []
+    for part in range(parts):
+        at = pl.ds(part * SUB, SUB)
+        copies = [
+            pltpu.make_async_copy(blocks_in.at[:, at, :], blocks.at[:, at, :], sems.at[part, 0]),
+            pltpu.make_async_copy(
+                faces_in.at[:, :, :, at, :], faces.at[:, :, :, at, :], sems.at[part, 1]
+            ),
+        ]
+        for copy in copies:
+            copy.start()
+        loads.append(copies)
+    lane = lane_index((SUB, LANES))
+    outs = []
+    for part in range(parts):
+        at = pl.ds(part * SUB, SUB)
+        loads[part][0].wait()
+        end = jnp.int32(0)
+        for group in range(groups):
+            start, end = end, end + widths[group]
+            tile, shift = start // LANES, start % LANES
+            keep = lane >= shift
+
+            def place(q, before):
+                to = pl.multiple_of(q * LANES, LANES)
+                here = pltpu.roll(blocks[group, at, pl.ds(to, LANES)], shift, 1)
+                one[tile + q, at, :] = jnp.where(keep, here, before)
+                return here
+
+            begin = one[tile, at, :]
+            tail = lax.fori_loop(0, capacity // LANES, place, begin, unroll=WINDOW)
+            one[tile + capacity // LANES, at, :] = tail
+        clear_edge(one, 2 * size_x, part)
+        clear_edge(two, 2 * size_x, part)
+        loads[part][1].wait()
+        for source, target in ((one, two), (two, one), (one, two), (two, result)):
+            diffuse_pass(source, target, face_x, face_y, size_x, part)
+        copies = by_level(out_to, result, out_sems, part, out=True)
+        for copy in copies:
+            copy.start()
+        outs += copies
+    for copy in outs:
+        copy.wait()
+
+
+def split_two(values):
+    high = values.astype(jnp.bfloat16)
+    low = (values - high.astype(jnp.float32)).astype(jnp.bfloat16)
+    return high, low
+
+
+def main_kernel(
+    chunks,
+    widths,
+    counts,
+    control_in,
+    diff_in,
+    raw,
+    perturb_in,
+    rinv_in,
+    vertical,
+    blocks,
+    faces_out,
+    faces,
+    control,
+    diff,
+    one,
+    two,
+    pieces,
+    slots,
+    column,
+    perturb,
+    rinv,
+    weight,
+    product,
+    from_core,
+    half,
+    from_z,
+    eighth,
+    from_x,
+    adjoint,
+    back,
+    field_sem,
+    load_sem,
+    in_send,
+    in_recv,
+    out_send,
+    out_recv,
+    core_send,
+    core_recv,
+    z_send,
+    z_recv,
+    x_send,
+    x_recv,
 ):
     groups, levels, capacity = pieces.shape
     size_x = control_in.shape[1]
     tiles = 2 * size_x
     parts = levels // SUB
-    diff_copies = [by_level(diff_in, diff, sems.at[0], part) for part in range(parts)]
-    control_copies = [by_level(control_in, control, sems.at[1], part) for part in range(parts)]
+    total = groups * levels
+    rows = capacity // chunks
+    face_x, face_y = faces.at[0], faces.at[1]
+    diff_copies = [by_level(diff_in, diff, field_sem.at[0], part) for part in range(parts)]
+    control_copies = [by_level(control_in, control, field_sem.at[1], part) for part in range(parts)]
     for part in range(parts):
         for copy in diff_copies[part] + control_copies[part]:
             copy.start()
-    clear_edge(control, size_x)
-    clear_edge(one, tiles)
-    clear_edge(two, tiles)
-    position = lax.axis_index("lev")
+    loads = [
+        pltpu.make_async_copy(perturb_in, perturb, load_sem.at[0]),
+        pltpu.make_async_copy(rinv_in, rinv, load_sem.at[1]),
+    ]
+    for copy in loads:
+        copy.start()
+
+    mem, lev = lax.axis_index("mem"), lax.axis_index("lev")
+    z, x_hi, core = mem // 4, lax.rem(mem // 2, 2), lax.rem(mem, 2)
+    other_core = (mem + 1 - 2 * core, lev)
+    other_x = (mem + 2 - 4 * x_hi, lev)
+    others_z = [lax.rem(z + d, 4) for d in range(1, 4)]
+    across_z = [(there * 4 + x_hi * 2 + core, lev) for there in others_z]
+    others_lev = [lax.rem(lev + d, groups) for d in range(1, groups)]
+    across_lev = [(mem, there) for there in others_lev]
+    sources = [lax.rem(lev + groups - d, groups) for d in range(1, groups)]
+    barrier = pltpu.get_barrier_semaphore()
+    everyone = [other_core, other_x] + across_z + across_lev
+    for device in everyone:
+        pl.semaphore_signal(barrier, 1, device_id=device, device_id_type=MESH)
+
     order = lax.broadcasted_iota(jnp.int32, raw.shape, 0) * LANES + lane_index(raw.shape)
-    code = lax.rem(raw[...], jnp.full(raw.shape, widths[position]))
-    slots[...] = jnp.where(order < counts[position], code, -1)
+    code = lax.rem(raw[...], jnp.full(raw.shape, widths[lev]))
+    slots[...] = jnp.where(order < counts[lev], code, -1)
     lane = lane_index((SUB, LANES))
-    for part in range(parts):
+
+    def smooth(part):
         at = pl.ds(part * SUB, SUB)
+        clear_edge(control, size_x, part)
+        clear_edge(one, tiles, part)
+        clear_edge(two, tiles, part)
         for copy in diff_copies[part]:
             copy.wait()
         make_faces(diff, face_x, face_y, size_x, part)
@@ -132,117 +256,6 @@
 
             lax.fori_loop(0, capacity // LANES, window, rolled(tile), unroll=WINDOW)
 
-
-def backward_kernel(
-    widths, blocks, diff_in, out_to, face_x, face_y, one, two, result, diff, sems
-):
-    groups, levels, capacity = blocks.shape
-    size_x = diff_in.shape[1]
-    parts = levels // SUB
-    diff_copies = [by_level(diff_in, diff, sems.at[0], part) for part in range(parts)]
-    for part in range(parts):
-        for copy in diff_copies[part]:
-            copy.start()
-    lane = lane_index((SUB, LANES))
-    for part in range(parts):
-        at = pl.ds(part * SUB, SUB)
-        end = jnp.int32(0)
-        for group in range(groups):
-            start, end = end, end + widths[group]
-            tile, shift = start // LANES, start % LANES
-            keep = lane >= shift
-
-            def place(q, before):
-                to = pl.multiple_of(q * LANES, LANES)
-                here = pltpu.roll(blocks[group, at, pl.ds(to, LANES)], shift, 1)
-                one[tile + q, at, :] = jnp.where(keep, here, before)
-                return here
-
-            begin = one[tile, at, :]
-            tail = lax.fori_loop(0, capacity // LANES, place, begin, unroll=WINDOW)
-            one[tile + capacity // LANES, at, :] = tail
-    clear_edge(one, 2 * size_x)
-    clear_edge(two, 2 * size_x)
-    outs = []
-    for part in range(parts):
-        for copy in diff_copies[part]:
-            copy.wait()
-        make_faces(diff, face_x, face_y, size_x, part)
-        for source, target in ((one, two), (two, one), (one, two), (two, result)):
-            diffuse_pass(source, target, face_x, face_y, size_x, part)
-        copies = by_level(out_to, result, sems.at[1], part, out=True)
-        for copy in copies:
-            copy.start()
-        outs += copies
-    for copy in outs:
-        copy.wait()
-
-
-def split_two(values):
-    high = values.astype(jnp.bfloat16)
-    low = (values - high.astype(jnp.float32)).astype(jnp.bfloat16)
-    return high, low
-
-
-def middle_kernel(
-    chunks,
-    pieces,
-    perturb_in,
-    rinv_in,
-    vertical,
-    slots,
-    blocks,
-    column,
-    perturb,
-    rinv,
-    weight,
-    product,
-    from_core,
-    half,
-    from_z,
-    eighth,
-    from_x,
-    adjoint,
-    back,
-    load_sem,
-    in_send,
-    in_recv,
-    out_send,
-    out_recv,
-    core_send,
-    core_recv,
-    z_send,
-    z_recv,
-    x_send,
-    x_recv,
-):
-    groups, levels, capacity = pieces.shape
-    total = groups * levels
-    rows = capacity // chunks
-    mem, lev = lax.axis_index("mem"), lax.axis_index("lev")
-    z, x_hi, core = mem // 4, lax.rem(mem // 2, 2), lax.rem(mem, 2)
-    other_core = (mem + 1 - 2 * core, lev)
-    other_x = (mem + 2 - 4 * x_hi, lev)
-    others_z = [lax.rem(z + d, 4) for d in range(1, 4)]
-    across_z = [(there * 4 + x_hi * 2 + core, lev) for there in others_z]
-    others_lev = [lax.rem(lev + d, groups) for d in range(1, groups)]
-    across_lev = [(mem, there) for there in others_lev]
-    sources = [lax.rem(lev + groups - d, groups) for d in range(1, groups)]
-
-    loads = [
-        pltpu.make_async_copy(perturb_in, perturb, load_sem.at[0]),
-        pltpu.make_async_copy(rinv_in, rinv, load_sem.at[1]),
-        pltpu.make_async_copy(pieces.at[lev], column.at[lev], load_sem.at[2]),
-    ]
-    for copy in loads:
-        copy.start()
-
-    barrier = pltpu.get_barrier_semaphore()
-    everyone = [other_core, other_x] + across_z + across_lev
-    for device in everyone:
-        pl.semaphore_signal(barrier, 1, device_id=device, device_id_type=MESH)
-    pl.semaphore_wait(barrier, len(everyone))
-
     pending = []
 
     def send(source, target, send_sem, recv_sem, device):
@@ -260,13 +273,14 @@
     def columns(k):
         return pl.ds(k * rows, rows)
 
-    def enter(k):
+    def enter(k, part):
+        at = pl.ds(part * SUB, SUB)
         for d in range(groups - 1):
             send(
-                pieces.at[others_lev[d], :, columns(k)],
-                column.at[lev, :, columns(k)],
-                in_send.at[k, d],
-                in_recv.at[k, d],
+                pieces.at[others_lev[d], at, columns(k)],
+                column.at[lev, at, columns(k)],
+                in_send.at[k, part, d],
+                in_recv.at[k, part, d],
                 across_lev[d],
             )
 
@@ -285,8 +299,16 @@
         )
         return dot(high, v_high) + (dot(high, v_low) + dot(low, v_high))
 
-    for k in range(min(PACE, chunks)):
-        enter(k)
+    for part in range(parts):
+        smooth(part)
+        if part == 0:
+            pl.semaphore_wait(barrier, len(everyone))
+        for k in range(min(PACE, chunks)):
+            enter(k, part)
+    loads.append(pltpu.make_async_copy(pieces.at[lev], column.at[lev], load_sem.at[2]))
+    loads.append(pltpu.make_async_copy(faces, faces_out, load_sem.at[3]))
+    for copy in loads[2:]:
+        copy.start()
 
     owned = rows // 16
     block = 512
@@ -322,10 +344,13 @@
     tile = 256
 
     def contract_in(k):
-        for d in range(groups - 1):
-            arrived(column.at[sources[d], :, columns(k)], in_recv.at[k, d])
+        for part in range(parts):
+            at = pl.ds(part * SUB, SUB)
+            for d in range(groups - 1):
+                arrived(column.at[sources[d], at, columns(k)], in_recv.at[k, part, d])
         if k + PACE < chunks:
-            enter(k + PACE)
+            for part in range(parts):
+                enter(k + PACE, part)
 
         def one(i, _):
             at = pl.ds(pl.multiple_of(k * rows + i * tile, tile), tile)
@@ -391,7 +416,7 @@
                 across_lev[d],
             )
         pltpu.make_async_copy(
-            back.at[lev, :, columns(k)], blocks.at[lev, :, columns(k)], load_sem.at[3 + k]
+            back.at[lev, :, columns(k)], blocks.at[lev, :, columns(k)], load_sem.at[4 + k]
         ).start()
 
     stages = dict(F=contract_in, A=add_core, B=add_z, C=add_x, D=give_z, E=give_core, G=contract_out)
@@ -404,8 +429,9 @@
         for d in range(groups - 1):
             arrived(blocks.at[sources[d], :, columns(k)], out_recv.at[k, d])
         pltpu.make_async_copy(
-            back.at[lev, :, columns(k)], blocks.at[lev, :, columns(k)], load_sem.at[3 + k]
+            back.at[lev, :, columns(k)], blocks.at[lev, :, columns(k)], load_sem.at[4 + k]
         ).wait()
+    loads[3].wait()
     for copy in pending:
         copy.wait_send()
 
@@ -425,26 +451,25 @@
     dma = pltpu.SemaphoreType.DMA
     lines = capacity // LANES
     wide = pltpu.VMEM((2 * size_x + lines + 2, levels, LANES), f32)
-    pieces, slots = pl.pallas_call(
-        forward_kernel,
+    rows = capacity // CHUNKS
+    both_faces = (2, size_x, 2, levels, LANES)
+    exchange = pltpu.VMEM((groups, levels, capacity), f32)
+    blocks, faces = pl.pallas_call(
+        functools.partial(main_kernel, CHUNKS),
         out_shape=(
             jax.ShapeDtypeStruct((groups, levels, capacity), f32),
-            jax.ShapeDtypeStruct((lines, LANES), jnp.int32),
+            jax.ShapeDtypeStruct(both_faces, f32),
         ),
-        in_specs=[SMEM, SMEM, ANY, ANY, VMEM],
-        out_specs=(VMEM, VMEM),
-        scratch_shapes=[field, field, field, wide, wide, field, dma((2, levels, 2))],
-        compiler_params=pltpu.CompilerParams(vmem_limit_bytes=LIMIT),
-        name="forward",
-    )(sub_widths, obs_counts, control[0], diffusivity, obs_raw.reshape(lines, LANES))
-
-    rows = capacity // CHUNKS
-    blocks = pl.pallas_call(
-        functools.partial(middle_kernel, CHUNKS),
-        out_shape=jax.ShapeDtypeStruct((groups, levels, capacity), f32),
-        in_specs=[ANY, ANY, ANY, VMEM, VMEM],
-        out_specs=VMEM,
+        in_specs=[SMEM, SMEM, ANY, ANY, VMEM, ANY, ANY, VMEM],
+        out_specs=(ANY, ANY),
         scratch_shapes=[
+            pltpu.VMEM(both_faces, f32),
+            field,
+            field,
+            wide,
+            wide,
+            exchange,
+            pltpu.VMEM((lines, LANES), jnp.int32),
             pltpu.VMEM((groups, levels, capacity), f32),
             pltpu.VMEM((capacity, LANES), f32),
             pltpu.VMEM((capacity, LANES), f32),
@@ -457,9 +482,10 @@
             pltpu.VMEM((CHUNKS, rows // 16, LANES), f32),
             pltpu.VMEM((capacity, LANES), f32),
             pltpu.VMEM((groups, levels, capacity), f32),
-            dma((3 + CHUNKS,)),
-            dma((CHUNKS, groups - 1)),
-            dma((CHUNKS, groups - 1)),
+            dma((2, levels, 2)),
+            dma((4 + CHUNKS,)),
+            dma((CHUNKS, levels // SUB, groups - 1)),
+            dma((CHUNKS, levels // SUB, groups - 1)),
             dma((CHUNKS, groups - 1)),
             dma((CHUNKS, groups - 1)),
             dma((2, CHUNKS)),
@@ -472,18 +498,35 @@
         compiler_params=pltpu.CompilerParams(
             vmem_limit_bytes=LIMIT, collective_id=0, has_side_effects=True
         ),
-        name="middle",
-    )(pieces, perturb[0], obs_rinv[0], vertical_filter, slots)
+        name="main",
+    )(
+        sub_widths,
+        obs_counts,
+        control[0],
+        diffusivity,
+        obs_raw.reshape(lines, LANES),
+        perturb[0],
+        obs_rinv[0],
+        vertical_filter,
+    )
 
     out = pl.pallas_call(
         backward_kernel,
         out_shape=jax.ShapeDtypeStruct((levels, size_x, size_y), f32),
-        in_specs=[SMEM, VMEM, ANY],
+        in_specs=[SMEM, ANY, ANY],
         out_specs=ANY,
-        scratch_shapes=[field, field, wide, wide, field, field, dma((2, levels, 2))],
+        scratch_shapes=[
+            pltpu.VMEM(both_faces, f32),
+            exchange,
+            wide,
+            wide,
+            field,
+            dma((levels // SUB, 2)),
+            dma((levels, 2)),
+        ],
         compiler_params=pltpu.CompilerParams(vmem_limit_bytes=LIMIT),
         name="backward",
-    )(sub_widths, blocks, diffusivity)
+    )(sub_widths, blocks, faces)
     return out.reshape(control.shape)
 
 

time: 120 us -> 111 us (0.925)
  Pallas kernels: 120 us -> 110 us
    pallas_call x2 -> x1, Pallas kernels: 106 us -> 97.4 us  [body(): pl.pallas_call(functools.partial(main_kernel, CHUNKS), out_shape=(jax.Sha...]
    pallas_call x1, Pallas kernels: 14.3 us -> 13 us  [body(): pl.pallas_call(backward_kernel, out_shape=jax.ShapeDtypeStruct((levels, s...]
where the time goes in v3:
time: 111 us; the launch traced here: 110 us
  Pallas kernels  110 us (99%)
    pallas_call x1, Pallas kernels, body(): pl.pallas_call(functools.partial(main_kernel, CHUNKS), out_shape=(jax.Sha...  97.4 us
    pallas_call x1, Pallas kernels, body(): pl.pallas_call(backward_kernel, out_shape=jax.ShapeDtypeStruct((levels, s...  13 us

profile of v3, /device:TPU:0, one launch (start us, length us, event | category | flops | bytes accessed | tf_op | source)
XLA Modules:
  0.0 110.4 jit_solution(7333412379322714268)
XLA Ops:
  0.0 97.4 %main.1 = (f32[8,16,6144]{2,1,0:T(8,128)}, f32[2,128,2,16,128]{4,3,2,1,0:T(8,128)}) custom-call(s32[8]{0:T(128)} %widths.3, s32[8]{0:T(128)} %counts.1, f32[16,128,256]{2,1,0:T(8,128)} %bitcast.7, f32[16,128,256]{2,1,0:T(8,128)} %diff_in.1, s32[48,128]{1,0:T(8,128)} %bitcast.8, f32[6144,128]{1,0:T(8,128)} %bitcast.5, f32[6144,128]{1,0:T(8,128)} %bitcast.6, ...), custom_call_target="tpu_custom_call" | custom-call | tf_op jit(solution)/shard_map/main/pallas_call | solution.py:457
  97.4 13.0 %backward.1 = f32[16,128,256]{2,1,0:T(8,128)} custom-call(s32[8]{0:T(128)} %widths.3, f32[8,16,6144]{2,1,0:T(8,128)} %get-tuple-element.7.blocks_in, f32[2,128,2,16,128]{4,3,2,1,0:T(8,128)} %get-tuple-element.8.faces_in), custom_call_target="tpu_custom_call" | custom-call | tf_op jit(solution)/shard_map/backward/pallas_call | solution.py:513

commit v4 on v3

--- a/solution.py
+++ b/solution.py
@@ -14,8 +14,9 @@
 
 
 CHUNKS = 8
-PACE = 2
-SCHED = (("F", 0), ("A", 0), ("B", 1), ("C", 2), ("D", 3), ("E", 4), ("G", 5))
+PACE = 3
+SCHED = (("F", 0), ("A", 0), ("B", 1), ("C", 3), ("E", 4), ("G", 5))
+EARLY = 9
 MESH = pl.DeviceIdType.MESH
 
 
@@ -310,9 +311,9 @@
     for copy in loads[2:]:
         copy.start()
 
-    owned = rows // 16
+    owned = rows // 8
     block = 512
-    first_row = core * (rows // 2) + z * (rows // 8) + x_hi * owned
+    first_row = core * (rows // 2) + z * owned
     here = jnp.concatenate(
         [
             first_row + k * rows + lax.broadcasted_iota(jnp.int32, (owned, LANES), 0)
@@ -333,11 +334,13 @@
             ],
             axis=1,
         )
-        dot = functools.partial(jnp.dot, preferred_element_type=jnp.float32)
-        weight[...] += dot(chosen, high) + dot(chosen, low)
+        both = jnp.concatenate([high, low], axis=1)
+        found = jnp.dot(chosen, both, preferred_element_type=jnp.float32)
+        weight[...] += found[:, :LANES] + found[:, LANES:]
         return 0
 
-    lax.fori_loop(0, capacity // block, gather, 0)
+    gathers = capacity // block
+    lax.fori_loop(0, EARLY, gather, 0)
     split = split_two(vertical[...])
     loads[0].wait()
     loads[2].wait()
@@ -374,19 +377,12 @@
             arrived(from_z.at[k, d], z_recv.at[0, k, d])
         own = half[k, pl.ds(pl.multiple_of(z * (rows // 8), 8), rows // 8), :]
         eighth[k] = (own + from_z[k, 0]) + (from_z[k, 1] + from_z[k, 2])
-        there = eighth.at[k, pl.ds(pl.multiple_of((1 - x_hi) * owned, 8), owned)]
-        send(there, from_x.at[k], x_send.at[0, k], x_recv.at[0, k], other_x)
+        send(eighth.at[k], from_x.at[k], x_send.at[k], x_recv.at[k], other_x)
 
     def add_x(k):
-        arrived(from_x.at[k], x_recv.at[0, k])
-        own = eighth[k, pl.ds(pl.multiple_of(x_hi * owned, 8), owned), :]
-        at = rows_at(k, (core, 2), (z, 4), (x_hi, 2))
-        adjoint[at, :] = (own + from_x[k]) * weight[k * owned : (k + 1) * owned, :]
-        send(adjoint.at[at], adjoint.at[at], x_send.at[1, k], x_recv.at[1, k], other_x)
-
-    def give_z(k):
-        arrived(adjoint.at[rows_at(k, (core, 2), (z, 4), (1 - x_hi, 2))], x_recv.at[1, k])
+        arrived(from_x.at[k], x_recv.at[k])
         at = rows_at(k, (core, 2), (z, 4))
+        adjoint[at, :] = (eighth[k] + from_x[k]) * weight[k * owned : (k + 1) * owned, :]
         for d in range(3):
             send(adjoint.at[at], adjoint.at[at], z_send.at[1, k, d], z_recv.at[1, k, d], across_z[d])
 
@@ -419,11 +415,13 @@
             back.at[lev, :, columns(k)], blocks.at[lev, :, columns(k)], load_sem.at[4 + k]
         ).start()
 
-    stages = dict(F=contract_in, A=add_core, B=add_z, C=add_x, D=give_z, E=give_core, G=contract_out)
+    stages = dict(F=contract_in, A=add_core, B=add_z, C=add_x, E=give_core, G=contract_out)
     for step in range(chunks + 6):
         for stage, lag in SCHED:
             if 0 <= step - lag < chunks:
                 stages[stage](step - lag)
+        if step == 0:
+            lax.fori_loop(EARLY, gathers, gather, 0)
 
     for k in range(chunks):
         for d in range(groups - 1):
@@ -473,13 +471,13 @@
             pltpu.VMEM((groups, levels, capacity), f32),
             pltpu.VMEM((capacity, LANES), f32),
             pltpu.VMEM((capacity, LANES), f32),
-            pltpu.VMEM((capacity // 16, LANES), f32),
+            pltpu.VMEM((capacity // 8, LANES), f32),
             pltpu.VMEM((capacity, LANES), f32),
             pltpu.VMEM((CHUNKS, rows // 2, LANES), f32),
             pltpu.VMEM((CHUNKS, rows // 2, LANES), f32),
             pltpu.VMEM((CHUNKS, 3, rows // 8, LANES), f32),
             pltpu.VMEM((CHUNKS, rows // 8, LANES), f32),
-            pltpu.VMEM((CHUNKS, rows // 16, LANES), f32),
+            pltpu.VMEM((CHUNKS, rows // 8, LANES), f32),
             pltpu.VMEM((capacity, LANES), f32),
             pltpu.VMEM((groups, levels, capacity), f32),
             dma((2, levels, 2)),
@@ -492,8 +490,8 @@
             dma((2, CHUNKS)),
             dma((2, CHUNKS, 3)),
             dma((2, CHUNKS, 3)),
-            dma((2, CHUNKS)),
-            dma((2, CHUNKS)),
+            dma((CHUNKS,)),
+            dma((CHUNKS,)),
         ],
         compiler_params=pltpu.CompilerParams(
             vmem_limit_bytes=LIMIT, collective_id=0, has_side_effects=True

time: 111 us -> 107 us (0.964)
  Pallas kernels: 110 us -> 106 us
    pallas_call x1, Pallas kernels: 97.4 us -> 92.7 us  [body(): pl.pallas_call(functools.partial(main_kernel, CHUNKS), out_shape=(jax.Sha...]
where the time goes in v4:
time: 107 us; the launch traced here: 106 us
  Pallas kernels  106 us (99%)
    pallas_call x1, Pallas kernels, body(): pl.pallas_call(functools.partial(main_kernel, CHUNKS), out_shape=(jax.Sha...  92.7 us
    pallas_call x1, Pallas kernels, body(): pl.pallas_call(backward_kernel, out_shape=jax.ShapeDtypeStruct((levels, s...  13 us

profile of v4, /device:TPU:0, one launch (start us, length us, event | category | flops | bytes accessed | tf_op | source)
XLA Modules:
  0.0 105.7 jit_solution(9724562433959105154)
XLA Ops:
  0.0 92.7 %main.1 = (f32[8,16,6144]{2,1,0:T(8,128)}, f32[2,128,2,16,128]{4,3,2,1,0:T(8,128)}) custom-call(s32[8]{0:T(128)} %widths.3, s32[8]{0:T(128)} %counts.1, f32[16,128,256]{2,1,0:T(8,128)} %bitcast.7, f32[16,128,256]{2,1,0:T(8,128)} %diff_in.1, s32[48,128]{1,0:T(8,128)} %bitcast.8, f32[6144,128]{1,0:T(8,128)} %bitcast.5, f32[6144,128]{1,0:T(8,128)} %bitcast.6, ...), custom_call_target="tpu_custom_call" | custom-call | tf_op jit(solution)/shard_map/main/pallas_call | solution.py:455
  92.7 13.0 %backward.1 = f32[16,128,256]{2,1,0:T(8,128)} custom-call(s32[8]{0:T(128)} %widths.3, f32[8,16,6144]{2,1,0:T(8,128)} %get-tuple-element.7.blocks_in, f32[2,128,2,16,128]{4,3,2,1,0:T(8,128)} %get-tuple-element.8.faces_in), custom_call_target="tpu_custom_call" | custom-call | tf_op jit(solution)/shard_map/backward/pallas_call | solution.py:511
